TPU v7x, 512 devices: a whole 4x4x16 slice. The times are simulated.
512 devices in a mesh: fsdp: 32 (over x, z_lo), member: 16 (over y, z_hi, core).
Axes of the slice: x: 4, y: 4, z: 16 (z_hi: 2, z_lo: 8; z = z_hi * 8 + z_lo), core: 2. Of those that a mesh axis runs over, the one named last changes fastest.
Arguments:
- frames: bfloat16 [16, 4608, 1536], P('member', 'fsdp'), may hold values from -6 to 6
- layer_norm_gain: float32 [1536], replicated, may hold values from 0.25 to 1.75
- input_projection: bfloat16 [1536, 6144], P('fsdp', 'member'), may hold values from -0.15625 to 0.15625
- output_projection: bfloat16 [6144, 1536], P('member', 'fsdp'), may hold values from -0.078125 to 0.078125
- adapter_down_map: bfloat16 [16, 1536, 64], P('member'), may hold values from -0.15625 to 0.15625
- adapter_up_map: bfloat16 [16, 64, 6144], P('member'), may hold values from -0.75 to 0.75
- lengths: int32 [16, 32], P('member', 'fsdp'), may hold values from 90 to 126, as said below
- cotangent: bfloat16 [16, 4608, 1536], P('member', 'fsdp'), may hold values from -0.29882812 to 0.29882812
Outputs:
- down_map_gradient: float32 [16, 1536, 64], P('member')
- up_map_gradient: float32 [16, 64, 6144], P('member')
Inputs may be any that keep to these rules, and one draw needn't show every extreme that they name: `lengths`: each member has at least one utterance of exactly 126 frames.
All inputs are finite; a program needn't handle non-finite values.
Results may differ from a plain program's by a relative error of at most 0.0058.
Values may be sent and summed in bfloat16 or wider, within the bound.
A program may use at most 128 MiB of HBM per device.

v0:
```python
import jax
import jax.numpy as jnp
from jax import lax
from jax.sharding import PartitionSpec as P

BUCKET = 144


def on_device(
    frames,
    layer_norm_gain,
    input_projection,
    output_projection,
    adapter_down_map,
    adapter_up_map,
    lengths,
    cotangent,
):
    members = lax.axis_size("member")
    values = frames[0].astype(jnp.float32)
    mean = jnp.mean(values, axis=1, keepdims=True)
    var = jnp.mean((values - mean) ** 2, axis=1, keepdims=True)
    normed_input = (layer_norm_gain * (values - mean) / jnp.sqrt(var + 1e-05)).astype(jnp.bfloat16)
    low_rank_state = jnp.dot(
        normed_input, adapter_down_map[0], preferred_element_type=jnp.float32
    ).astype(jnp.bfloat16)
    positions = jnp.arange(BUCKET, dtype=jnp.int32)
    mask = (positions[None, :] < lengths[0][:, None]).reshape(-1)
    masked = cotangent[0] * mask.astype(cotangent.dtype)[:, None]
    rows = normed_input.shape[0]
    up_map_slices = lax.all_to_all(
        adapter_up_map, "member", split_axis=2, concat_axis=0, tiled=True
    )
    stacked_norm, stacked_low, stacked_grad = (
        lax.all_gather(normed_input, "member", axis=0, tiled=True),
        lax.all_gather(low_rank_state, "member", axis=0, tiled=True),
        lax.all_gather(masked, "member", axis=0, tiled=True),
    )
    low_rank_blocks = stacked_low.reshape(members, rows, -1)
    adapter_term = jnp.einsum(
        "dgs,dsb->dgb", low_rank_blocks, up_map_slices, preferred_element_type=jnp.float32
    )
    adapter_term = adapter_term.reshape(members * rows, -1)
    columns = stacked_norm
    pre = adapter_term + jnp.dot(
        columns,
        lax.all_gather(input_projection, "fsdp", axis=0, tiled=True),
        preferred_element_type=jnp.float32,
    )
    columns = stacked_grad
    dhid = 0.5 * lax.dot_general(
        columns,
        lax.all_gather(output_projection, "fsdp", axis=1, tiled=True),
        (((1,), (1,)), ((), ())),
        preferred_element_type=jnp.float32,
    )
    sigma = jax.nn.sigmoid(pre)
    dpre = (dhid * sigma * (1.0 + pre * (1.0 - sigma))).astype(jnp.bfloat16)
    preact_gradient_blocks = dpre.reshape(members, rows, -1)
    up_partial = jnp.einsum(
        "jnz,jnv->jzv", low_rank_blocks, preact_gradient_blocks, preferred_element_type=jnp.float32
    )
    back_partial = jnp.einsum(
        "yha,ywa->yhw", preact_gradient_blocks, up_map_slices, preferred_element_type=jnp.float32
    )
    back = lax.psum_scatter(back_partial, "member", scatter_dimension=0, tiled=True)[0].astype(
        jnp.bfloat16
    )
    down_partial = jnp.dot(normed_input.T, back, preferred_element_type=jnp.float32)
    up_summed = lax.psum(up_partial, "fsdp")
    up_map_gradient = lax.all_to_all(up_summed, "member", split_axis=0, concat_axis=2, tiled=True)
    down_map_gradient = lax.psum(down_partial, "fsdp")
    return (down_map_gradient[None], up_map_gradient)


def solution(mesh):
    in_specs = (
        P("member", "fsdp", None),
        P(),
        P("fsdp", "member"),
        P("member", "fsdp"),
        P("member", None, None),
        P("member", None, None),
        P("member", "fsdp"),
        P("member", "fsdp", None),
    )
    out_specs = (P("member", None, None), P("member", None, None))
    return jax.shard_map(
        on_device, mesh=mesh, in_specs=in_specs, out_specs=out_specs, check_vma=False
    )
```

profile of v0, /device:TPU:1, one launch (start us, length us, event | category | flops | bytes accessed | tf_op | source)
XLA Modules:
  0.0 1449.9 jit_solution(2812259246271979070)
XLA Ops:
  7.2 0.0 copy-start
  7.2 0.0 all-gather.12.cloned.1.call-start
  7.2 0.7 all-gather.12.cloned.1.call-update
  7.9 0.0 all-gather.10.cloned.1.call-start
  8.0 1.2 convert_reduce_fusion
  9.1 1.3 fusion.10
  10.4 2.0 fusion.12
  12.4 0.0 all-gather.10.cloned.1.call-update
  12.5 0.0 all-gather.8.cloned.1.call-start
  12.5 0.7 all-gather.8.cloned.1.call-update
  13.2 0.0 all-gather.6.cloned.1.call-start
  13.9 1.9 bitcast_multiply_fusion
  15.8 0.0 all-gather.6.cloned.1.call-update
  15.8 6.7 copy.12
  22.5 0.5 broadcast.58
  23.0 34.4 %reduce.1 = bf16[6144,64]{1,0:T(8,128)(2,1)} reduce(bf16[6144,1,64]{2,1,0:T(2,128)(2,1)S(1)} %bitcast.57, bf16[]{:T(256)} %broadcast.58), dimensions={1}, to_apply=%bitcast.44.reduce_sub_computation | reduce | bytes 1572866
  57.5 3.9 reshape.87
  61.4 19.2 %all-to-all-start = ((bf16[16,2,12288]{2,1,0:T(2,128)(2,1)}), bf16[16,2,12288]{2,1,0:T(2,128)(2,1)}, u32[]{:S(2)}, u32[]{:S(2)}) async-start(bf16[16,2,12288]{2,1,0:T(2,128)(2,1)} %reshape.87), calls=%async_computation | async-start | bytes 1572864 | tf_op jit(solution)/shard_map/all_to_all | solution.py:31
  80.6 0.0 reduce-scatter.2.cloned.1.call-start
  80.7 0.2 fusion.17
  80.9 0.0 copy-start.3
  80.9 0.7 copy-done.3
  81.7 0.3 fusion.3
  81.9 75.8 %all-gather = bf16[16,144,64]{1,2,0:T(8,128)(2,1)} all-gather(bf16[1,144,64]{1,2,0:T(8,128)(2,1)S(1)} %fusion.3), channel_id=1, replica_groups=mesh['fsdp'=32,'member'=16] {'member'}, dimensions={0}, use_global_device_ids=true | all-gather | bytes 313344 | tf_op jit(solution)/shard_map/all_gather | solution.py:36
  157.8 0.0 all-to-all-done
  157.8 4.6 reshape.88
  162.3 1.3 copy.18
  163.7 1.7 copy.14
  165.4 3.5 fusion.15
  168.9 70.4 %all-gather.12.cloned.1.call-done = bf16[1536,384]{1,0:T(8,128)(2,1)} async-done(((bf16[48,384]{1,0:T(8,128)(2,1)}), bf16[1536,384]{1,0:T(8,128)(2,1)}) %all-gather.12.cloned.1.call-update) | async-done | bytes 1179664 | tf_op jit(solution)/shard_map/all_gather | solution.py:47
  239.3 179.4 %all-gather.10.cloned.1.call-done = bf16[2304,1536]{1,0:T(8,128)(2,1)} async-done(((bf16[144,1536]{1,0:T(8,128)(2,1)}), bf16[2304,1536]{1,0:T(8,128)(2,1)}) %all-gather.10.cloned.1.call-update) | async-done | bytes 7077904 | tf_op jit(solution)/shard_map/all_gather | solution.py:35
  418.7 10.0 convolution_add_fusion
  428.7 184.5 %all-gather.8.cloned.1.call-done = bf16[384,1536]{0,1:T(8,128)(2,1)} async-done(((bf16[384,48]{0,1:T(8,128)(2,1)}), bf16[384,1536]{0,1:T(8,128)(2,1)}) %all-gather.8.cloned.1.call-update) | async-done | bytes 1179664 | tf_op jit(solution)/shard_map/all_gather | solution.py:53
  613.2 183.5 %all-gather.6.cloned.1.call-done = bf16[2304,1536]{1,0:T(8,128)(2,1)} async-done(((bf16[144,1536]{1,0:T(8,128)(2,1)}), bf16[2304,1536]{1,0:T(8,128)(2,1)}) %all-gather.6.cloned.1.call-update) | async-done | bytes 7077904 | tf_op jit(solution)/shard_map/all_gather | solution.py:37
  796.6 9.0 fusion.2
  805.6 0.0 copy-start.2
  805.6 1.9 fusion.13
  807.5 0.0 reduce-scatter.2.cloned.1.call-update
  807.5 0.0 all-reduce.3.cloned.1.call-start
  807.6 0.0 copy-done.2
  807.6 1.6 fusion.21
  809.2 94.6 %reduce-scatter.2.cloned.1.call-done = f32[1,144,64]{1,2,0:T(8,128)} async-done(((f32[16,144,64]{1,2,0:T(8,128)}), f32[1,144,64]{1,2,0:T(8,128)}) %reduce-scatter.2.cloned.1.call-update) | async-done | bytes 36880 | tf_op jit(solution)/shard_map/reduce_scatter | solution.py:66
  903.9 1.8 convolution_bitcast_fusion
  905.7 0.0 all-reduce.3.cloned.1.call-update
  905.7 434.8 %all-reduce.3.cloned.1.call-done = (f32[1,1536,64]{1,2,0:T(8,128)}, f32[16,64,384]{2,1,0:T(8,128)}) async-done(((f32[1,1536,64]{1,2,0:T(8,128)}, f32[16,64,384]{2,1,0:T(8,128)}), (f32[1,1536,64]{1,2,0:T(8,128)}, f32[16,64,384]{2,1,0:T(8,128)})) %all-reduce.3.cloned.1.call-update) | async-done | bytes 1966096 | tf_op jit(solution)/shard_map/psum | solution.py:72
  1340.4 100.6 %all_to_all.36 = f32[16,64,384]{2,1,0:T(8,128)S(1)} all-to-all(f32[16,64,384]{2,1,0:T(8,128)} %get-tuple-element.3), channel_id=1, replica_groups=mesh['fsdp'=32,'member'=16] {'member'}, dimensions={0} | all-to-all | bytes 3145728 | tf_op jit(solution)/shard_map/all_to_all | solution.py:71
  1441.0 1.2 copy.19
  1442.3 0.7 copy.23
  (12 shorter events, 0.0 us)
Async XLA Ops:
  7.2 74.5 %copy-start = (bf16[1,1536,64]{1,2,0:T(8,128)(2,1)S(1)}, bf16[1,1536,64]{1,2,0:T(8,128)(2,1)}, u32[]{:S(2)}) copy-start(bf16[1,1536,64]{1,2,0:T(8,128)(2,1)} %param.12) | copy-start | bytes 589828
  7.2 232.1 %all-gather.12.cloned.1.call-start = ((), (), s32[]{:S(2)}) async-start(), calls=%async_computation.6 | async-start | bytes 1216512 | tf_op jit(solution)/shard_map/all_gather | solution.py:47
  7.9 410.8 %all-gather.10.cloned.1.call-start = ((), (), s32[]{:S(2)}) async-start(), calls=%async_computation.5 | async-start | bytes 7520256 | tf_op jit(solution)/shard_map/all_gather | solution.py:35
  12.5 600.7 %all-gather.8.cloned.1.call-start = ((), (), s32[]{:S(2)}) async-start(), calls=%async_computation.4 | async-start | bytes 1216512 | tf_op jit(solution)/shard_map/all_gather | solution.py:53
  13.2 783.4 %all-gather.6.cloned.1.call-start = ((), (), s32[]{:S(2)}) async-start(), calls=%async_computation.3 | async-start | bytes 7520256 | tf_op jit(solution)/shard_map/all_gather | solution.py:37
  23.0 57.6 %copy-start.6 = (f32[1536]{0:T(1024)S(1)}, f32[1536]{0:T(1024)}, u32[]{:S(2)}) copy-start(f32[1536]{0:T(1024)} %param.9) | copy-start | bytes 18436
  57.5 23.2 %copy-start.1 = (bf16[1,144,1536]{2,1,0:T(8,128)(2,1)S(1)}, bf16[1,144,1536]{2,1,0:T(8,128)(2,1)}, u32[]{:S(2)}) copy-start(bf16[1,144,1536]{2,1,0:T(8,128)(2,1)} %param.8) | copy-start | bytes 1327108
  61.4 96.4 %all-to-all-start = ((bf16[16,2,12288]{2,1,0:T(2,128)(2,1)}), bf16[16,2,12288]{2,1,0:T(2,128)(2,1)}, u32[]{:S(2)}, u32[]{:S(2)}) async-start(bf16[16,2,12288]{2,1,0:T(2,128)(2,1)} %reshape.87), calls=%async_computation | async-start | bytes 1572864 | tf_op jit(solution)/shard_map/all_to_all | solution.py:31
  80.6 823.2 %reduce-scatter.2.cloned.1.call-start = ((), (), s32[]{:S(2)}) async-start(), calls=%async_computation.7 | async-start | bytes 1114112 | tf_op jit(solution)/shard_map/reduce_scatter | solution.py:66
  80.9 0.8 copy-start.3
  805.6 2.0 copy-start.2
  807.5 96.3 %copy-start.4 = (bf16[144,1536]{1,0:T(8,128)(2,1)S(1)}, bf16[144,1536]{1,0:T(8,128)(2,1)}, u32[]{:S(2)}) copy-start(bf16[144,1536]{1,0:T(8,128)(2,1)} %copy-done.3) | copy-start | bytes 1327108
  807.5 532.9 %all-reduce.3.cloned.1.call-start = ((), (), s32[]{:S(2)}) async-start(), calls=%async_computation.8 | async-start | bytes 3932160 | tf_op jit(solution)/shard_map/psum | solution.py:72
  1340.4 101.8 %copy-start.5 = (f32[1,1536,64]{1,2,0:T(8,128)S(1)}, f32[1,1536,64]{1,2,0:T(8,128)}, u32[]{:S(2)}) copy-start(f32[1,1536,64]{1,2,0:T(8,128)} %get-tuple-element.4) | copy-start | bytes 1179652
Sparse Core Ops, SparseCore 0:
  10.1 229.1 all-gather.11
  242.5 176.1 all-gather.9
  420.8 192.3 all-gather.7
  616.3 180.3 all-gather.5
  807.7 96.1 reduce-scatter.1
  907.6 432.8 all-reduce.2
where the time goes:
time: 1450 us
  waiting for transfers between devices  1150 us (79%)
  blocking collectives  176 us (12%)
  other arithmetic  41.1 us (3%)
  matrix products  28 us (2%)
  local copies, waits for them, and re-layouts  21.5 us (1%)
  starting transfers between devices  19.5 us (1%)
  between operations  14.9 us (1%)
    psum x1, waiting for transfers between devices, on_device(): down_map_gradient = lax.psum(down_partial, 'fsdp')  435 us
    all_gather x1, waiting for transfers between devices, on_device(): lax.all_gather(output_projection, 'fsdp', axis=1, tiled=True)  184 us
    all_gather x1, waiting for transfers between devices, on_device(): lax.all_gather(masked, 'member', axis=0, tiled=True)  183 us
    all_gather x1, waiting for transfers between devices, on_device(): lax.all_gather(normed_input, 'member', axis=0, tiled=True)  179 us
    all_to_all x1, blocking collectives, on_device(): lax.all_to_all(up_summed, 'member', split_axis=0, concat_axis=2, tiled=True)  101 us
    reduce_scatter x1, waiting for transfers between devices, on_device(): lax.psum_scatter(back_partial, 'member', scatter_dimension=0, tiled=True)[0]  94.6 us
    all_gather x1, blocking collectives, on_device(): lax.all_gather(low_rank_state, 'member', axis=0, tiled=True)  75.8 us
    all_gather x1, waiting for transfers between devices, on_device(): lax.all_gather(input_projection, 'fsdp', axis=0, tiled=True)  70.4 us
  transfers between devices with their start and end apart: 7, of which 6 were waited for; matrix products, arithmetic and copies ran while one was open for 5% of the time, Pallas kernels for 0%

commit v1 on v0

--- a/solution.py
+++ b/solution.py
@@ -1,9 +1,18 @@
+import functools
 import jax
 import jax.numpy as jnp
 from jax import lax
 from jax.sharding import PartitionSpec as P
 
 BUCKET = 144
+
+
+def post_knots(patch, lane_axis):
+    ready = jnp.sum(lax.all_gather(patch, axis_name=lane_axis), 0)
+    return ready
+
+
+_spread_object = functools.partial(post_knots, lane_axis="fsdp")
 
 
 def on_device(
@@ -69,7 +78,7 @@
     down_partial = jnp.dot(normed_input.T, back, preferred_element_type=jnp.float32)
     up_summed = lax.psum(up_partial, "fsdp")
     up_map_gradient = lax.all_to_all(up_summed, "member", split_axis=0, concat_axis=2, tiled=True)
-    down_map_gradient = lax.psum(down_partial, "fsdp")
+    down_map_gradient = _spread_object(down_partial)
     return (down_map_gradient[None], up_map_gradient)
 
 

time: 1450 us -> 1730 us (1.19)
  waiting for transfers between devices: 1150 us -> 1390 us
  blocking collectives: 176 us -> 194 us
    all_gather x0 -> x1, waiting for transfers between devices: none -> 242 us  [post_knots(): ready = jnp.sum(lax.all_gather(patch, axis_name=lane_axis), 0)]
    all_to_all x1, blocking collectives: 101 us -> 118 us  [on_device(): lax.all_to_all(up_summed, 'member', split_axis=0, concat_axis=2, tiled=True)]
  transfers between devices with their start and end apart: 7 -> 8, of which waited for: 6 -> 7; matrix products, arithmetic and copies ran while one was open for 5% -> 5% of each run, Pallas kernels for 0% -> 0%
where the time goes in v1:
time: 1730 us
  waiting for transfers between devices  1390 us (80%)
  blocking collectives  194 us (11%)
  other arithmetic  48.5 us (3%)
  local copies, waits for them, and re-layouts  36.9 us (2%)
  matrix products  28 us (2%)
  starting transfers between devices  19.5 us (1%)
    psum x1, waiting for transfers between devices, on_device(): up_summed = lax.psum(up_partial, 'fsdp')  434 us
    all_gather x1, waiting for transfers between devices, post_knots(): ready = jnp.sum(lax.all_gather(patch, axis_name=lane_axis), 0)  242 us
    all_gather x1, waiting for transfers between devices, on_device(): lax.all_gather(output_projection, 'fsdp', axis=1, tiled=True)  184 us
    all_gather x1, waiting for transfers between devices, on_device(): lax.all_gather(masked, 'member', axis=0, tiled=True)  183 us
    all_gather x1, waiting for transfers between devices, on_device(): lax.all_gather(normed_input, 'member', axis=0, tiled=True)  182 us
    all_to_all x1, blocking collectives, on_device(): lax.all_to_all(up_summed, 'member', split_axis=0, concat_axis=2, tiled=True)  118 us
    reduce_scatter x1, waiting for transfers between devices, on_device(): lax.psum_scatter(back_partial, 'member', scatter_dimension=0, tiled=True)[0]  94.5 us
    all_gather x1, blocking collectives, on_device(): lax.all_gather(low_rank_state, 'member', axis=0, tiled=True)  75.8 us
  transfers between devices with their start and end apart: 8, of which 7 were waited for; matrix products, arithmetic and copies ran while one was open for 5% of the time, Pallas kernels for 0%

profile of v1, /device:TPU:1, one launch (start us, length us, event | category | flops | bytes accessed | tf_op | source)
XLA Modules:
  0.0 1733.2 jit_solution(4648620251917834198)
XLA Ops:
  7.2 0.0 copy-start
  7.2 0.0 all-gather.14.cloned.1.call-start
  7.2 0.7 all-gather.14.cloned.1.call-update
  7.9 0.0 all-gather.12.cloned.1.call-start
  8.0 1.2 convert_reduce_fusion
  9.1 1.3 fusion.10
  10.4 2.0 fusion.12
  12.4 0.0 all-gather.12.cloned.1.call-update
  12.4 0.0 all-gather.10.cloned.1.call-start
  12.5 0.7 all-gather.10.cloned.1.call-update
  13.2 0.0 all-gather.8.cloned.1.call-start
  13.9 1.9 bitcast_multiply_fusion
  15.8 0.0 all-gather.8.cloned.1.call-update
  15.8 6.7 copy.12
  22.5 0.5 broadcast.58
  23.0 34.4 %reduce.1 = bf16[6144,64]{1,0:T(8,128)(2,1)} reduce(bf16[6144,1,64]{2,1,0:T(2,128)(2,1)S(1)} %bitcast.62, bf16[]{:T(256)} %broadcast.58), dimensions={1}, to_apply=%bitcast.48.reduce_sub_computation | reduce | bytes 1572866
  57.5 3.9 reshape.88
  61.4 19.2 %all-to-all-start = ((bf16[16,2,12288]{2,1,0:T(2,128)(2,1)}), bf16[16,2,12288]{2,1,0:T(2,128)(2,1)}, u32[]{:S(2)}, u32[]{:S(2)}) async-start(bf16[16,2,12288]{2,1,0:T(2,128)(2,1)} %reshape.88), calls=%async_computation | async-start | bytes 1572864 | tf_op jit(solution)/shard_map/all_to_all | solution.py:40
  80.6 0.0 reduce-scatter.2.cloned.1.call-start
  80.7 0.2 fusion.17
  80.9 0.7 copy-done.4
  81.6 0.3 fusion.3
  81.9 75.8 %all-gather.1 = bf16[16,144,64]{1,2,0:T(8,128)(2,1)} all-gather(bf16[1,144,64]{1,2,0:T(8,128)(2,1)S(1)} %fusion.3), channel_id=1, replica_groups=mesh['fsdp'=32,'member'=16] {'member'}, dimensions={0}, use_global_device_ids=true | all-gather | bytes 313344 | tf_op jit(solution)/shard_map/all_gather | solution.py:45
  157.7 4.6 reshape.89
  162.2 1.3 copy.18
  163.6 1.7 copy.14
  165.3 3.5 fusion.15
  168.8 69.3 %all-gather.14.cloned.1.call-done = bf16[1536,384]{1,0:T(8,128)(2,1)} async-done(((bf16[48,384]{1,0:T(8,128)(2,1)}), bf16[1536,384]{1,0:T(8,128)(2,1)}) %all-gather.14.cloned.1.call-update) | async-done | bytes 1179664 | tf_op jit(solution)/shard_map/all_gather | solution.py:56
  238.1 181.8 %all-gather.12.cloned.1.call-done = bf16[2304,1536]{1,0:T(8,128)(2,1)} async-done(((bf16[144,1536]{1,0:T(8,128)(2,1)}), bf16[2304,1536]{1,0:T(8,128)(2,1)}) %all-gather.12.cloned.1.call-update) | async-done | bytes 7077904 | tf_op jit(solution)/shard_map/all_gather | solution.py:44
  419.8 10.0 convolution_add_fusion
  429.8 184.5 %all-gather.10.cloned.1.call-done = bf16[384,1536]{0,1:T(8,128)(2,1)} async-done(((bf16[384,48]{0,1:T(8,128)(2,1)}), bf16[384,1536]{0,1:T(8,128)(2,1)}) %all-gather.10.cloned.1.call-update) | async-done | bytes 1179664 | tf_op jit(solution)/shard_map/all_gather | solution.py:62
  614.3 183.5 %all-gather.8.cloned.1.call-done = bf16[2304,1536]{1,0:T(8,128)(2,1)} async-done(((bf16[144,1536]{1,0:T(8,128)(2,1)}), bf16[2304,1536]{1,0:T(8,128)(2,1)}) %all-gather.8.cloned.1.call-update) | async-done | bytes 7077904 | tf_op jit(solution)/shard_map/all_gather | solution.py:46
  797.8 9.0 fusion.2
  806.8 1.9 fusion.13
  808.6 0.0 reduce-scatter.2.cloned.1.call-update
  808.7 0.0 all-reduce.2.cloned.1.call-start
  808.7 1.6 fusion.22
  810.3 0.0 all-reduce.2.cloned.1.call-update
  810.4 0.0 all-gather.16.cloned.1.call-start
  810.4 94.5 %reduce-scatter.2.cloned.1.call-done = f32[1,144,64]{1,2,0:T(8,128)} async-done(((f32[16,144,64]{1,2,0:T(8,128)}), f32[1,144,64]{1,2,0:T(8,128)}) %reduce-scatter.2.cloned.1.call-update) | async-done | bytes 36880 | tf_op jit(solution)/shard_map/reduce_scatter | solution.py:75
  904.9 1.8 fusion.19
  906.7 0.0 all-gather.16.cloned.1.call-update
  906.8 433.9 %all-reduce.2.cloned.1.call-done = f32[16,64,384]{2,1,0:T(8,128)} async-done(((f32[16,64,384]{2,1,0:T(8,128)}), f32[16,64,384]{2,1,0:T(8,128)}) %all-reduce.2.cloned.1.call-update) | async-done | bytes 1572880 | tf_op jit(solution)/shard_map/psum | solution.py:79
  1340.6 118.5 %all_to_all.36 = f32[16,64,384]{2,1,0:T(8,128)S(1)} all-to-all(f32[16,64,384]{2,1,0:T(8,128)} %all-reduce.2.cloned.1.call-done), channel_id=1, replica_groups=mesh['fsdp'=32,'member'=16] {'member'}, dimensions={0} | all-to-all | bytes 3145728 | tf_op jit(solution)/shard_map/all_to_all | solution.py:80
  1459.1 1.2 copy.19
  1460.4 242.4 %all-gather.16.cloned.1.call-done = f32[49152,64]{0,1:T(8,128)} async-done(((f32[1536,64]{0,1:T(8,128)}), f32[49152,64]{0,1:T(8,128)}) %all-gather.16.cloned.1.call-update) | async-done | bytes 12582928 | tf_op jit(solution)/shard_map/all_gather | solution.py:11
  1702.7 16.2 copy.20
  1718.9 7.5 bitcast_reduce_fusion
  (16 shorter events, 0.0 us)
Async XLA Ops:
  7.2 74.5 %copy-start = (bf16[1,1536,64]{1,2,0:T(8,128)(2,1)S(1)}, bf16[1,1536,64]{1,2,0:T(8,128)(2,1)}, u32[]{:S(2)}) copy-start(bf16[1,1536,64]{1,2,0:T(8,128)(2,1)} %param.12) | copy-start | bytes 589828
  7.2 230.9 %all-gather.14.cloned.1.call-start = ((), (), s32[]{:S(2)}) async-start(), calls=%async_computation.6 | async-start | bytes 1216512 | tf_op jit(solution)/shard_map/all_gather | solution.py:56
  7.9 411.9 %all-gather.12.cloned.1.call-start = ((), (), s32[]{:S(2)}) async-start(), calls=%async_computation.5 | async-start | bytes 7520256 | tf_op jit(solution)/shard_map/all_gather | solution.py:44
  12.4 601.8 %all-gather.10.cloned.1.call-start = ((), (), s32[]{:S(2)}) async-start(), calls=%async_computation.4 | async-start | bytes 1216512 | tf_op jit(solution)/shard_map/all_gather | solution.py:62
  13.2 784.6 %all-gather.8.cloned.1.call-start = ((), (), s32[]{:S(2)}) async-start(), calls=%async_computation.3 | async-start | bytes 7520256 | tf_op jit(solution)/shard_map/all_gather | solution.py:46
  23.0 57.6 %copy-start.6 = (f32[1536]{0:T(1024)S(1)}, f32[1536]{0:T(1024)}, u32[]{:S(2)}) copy-start(f32[1536]{0:T(1024)} %param.9) | copy-start | bytes 18436
  57.5 23.2 %copy-start.2 = (bf16[1,144,1536]{2,1,0:T(8,128)(2,1)S(1)}, bf16[1,144,1536]{2,1,0:T(8,128)(2,1)}, u32[]{:S(2)}) copy-start(bf16[1,144,1536]{2,1,0:T(8,128)(2,1)} %param.8) | copy-start | bytes 1327108
  61.4 96.3 %all-to-all-start = ((bf16[16,2,12288]{2,1,0:T(2,128)(2,1)}), bf16[16,2,12288]{2,1,0:T(2,128)(2,1)}, u32[]{:S(2)}, u32[]{:S(2)}) async-start(bf16[16,2,12288]{2,1,0:T(2,128)(2,1)} %reshape.88), calls=%async_computation | async-start | bytes 1572864 | tf_op jit(solution)/shard_map/all_to_all | solution.py:40
  80.6 824.4 %reduce-scatter.2.cloned.1.call-start = ((), (), s32[]{:S(2)}) async-start(), calls=%async_computation.7 | async-start | bytes 1114112 | tf_op jit(solution)/shard_map/reduce_scatter | solution.py:75
  80.9 0.7 copy-start.4
  806.8 1.9 copy-start.3
  808.6 96.3 %copy-start.5 = (bf16[144,1536]{1,0:T(8,128)(2,1)S(1)}, bf16[144,1536]{1,0:T(8,128)(2,1)}, u32[]{:S(2)}) copy-start(bf16[144,1536]{1,0:T(8,128)(2,1)} %copy-done.4) | copy-start | bytes 1327108
  808.7 532.0 %all-reduce.2.cloned.1.call-start = ((), (), s32[]{:S(2)}) async-start(), calls=%async_computation.8 | async-start | bytes 3145728 | tf_op jit(solution)/shard_map/psum | solution.py:79
  810.4 892.4 %all-gather.16.cloned.1.call-start = ((), (), s32[]{:S(2)}) async-start(), calls=%async_computation.9 | async-start | bytes 12976128 | tf_op jit(solution)/shard_map/all_gather | solution.py:11
  1702.7 23.7 %copy-start.1 = (bf16[1,1536,64]{1,2,0:T(8,128)(2,1)S(1)}, bf16[1,1536,64]{1,2,0:T(8,128)(2,1)}, u32[]{:S(2)}) copy-start(bf16[1,1536,64]{1,2,0:T(8,128)(2,1)} %param.12) | copy-start | bytes 589828
Sparse Core Ops, SparseCore 0:
  10.1 227.9 all-gather.13
  241.3 178.4 all-gather.11
  421.9 192.3 all-gather.9
  617.4 180.3 all-gather.7
  808.8 96.1 reduce-scatter.1
  908.5 432.0 all-reduce.1
  1343.3 359.3 all-gather.15
